TPU v7x, 32 devices: a whole 2x2x4 slice. The times are simulated.
32 devices in a mesh: group: 4 (over z), tensor: 4 (over y, core), role: 2 (over x).
Axes of the slice: x: 2, y: 2, z: 4, core: 2. Of those that a mesh axis runs over, the one named last changes fastest.
Arguments:
- queries: bfloat16 [4096, 4096], P(('group', 'role'), 'tensor'), may hold values from -8 to 8
- keys_values: bfloat16 [2, 4096, 1024], P(None, ('group', 'role')), may hold values from -8 to 8
- doc_ids: int32 [4096], P(('group', 'role')), may hold values from 0 to 15, never falling along the last dimension, each value on 1 to 1024 neighbouring positions
Outputs:
- attended: bfloat16 [4096, 4096], P(('group', 'role'), 'tensor')
All inputs are finite; a program needn't handle non-finite values.
Results may differ from a plain program's by a relative error of at most 0.0036.
Values may be sent and summed in bfloat16 or wider, within the bound.
A program may use at most 64 MiB of HBM per device.

v0:
```python
import math
import jax
import jax.numpy as jnp
from jax import lax
from jax.sharding import PartitionSpec as P

HEADS = 32
KV_HEADS = 8
HD = 128


def absorb_keys(running, scores, visible, values, pattern):
    largest, totals, summed = running
    masked = jnp.where(visible, scores, -1e30)
    newest = jnp.maximum(largest, jnp.max(masked, axis=-1))
    factor = jnp.exp(largest - newest)
    weights = jnp.where(visible, jnp.exp(masked - newest[..., None]), 0.0)
    totals = totals * factor + jnp.sum(weights, axis=-1)
    rounded = weights.astype(jnp.bfloat16)
    summed = summed * factor[..., None] + jnp.einsum(
        pattern, rounded, values, preferred_element_type=jnp.float32
    )
    return (newest, totals, summed)


def head_attention(queries, keys_values, doc_ids):
    tok_rows, width_here = queries.shape
    role_index = lax.axis_index("role")
    tensor_index = lax.axis_index("tensor")
    heads_here = width_here // HD
    group_width = HEADS // KV_HEADS
    scaling = 1.0 / math.sqrt(HD)
    kv_count = max(1, heads_here // group_width)
    share = heads_here // kv_count
    first_kv = tensor_index * heads_here // group_width
    own_kv = lax.dynamic_slice_in_dim(keys_values, first_kv * HD, kv_count * HD, 2)[None]
    local_q = queries.reshape(tok_rows, kv_count, share, HD)
    query_pos = role_index * tok_rows + jnp.arange(tok_rows, dtype=jnp.int32)
    row_steps = jnp.arange(tok_rows, dtype=jnp.int32)
    start_state = (
        jnp.full((tok_rows, kv_count, share), -1e30, jnp.float32),
        jnp.zeros((tok_rows, kv_count, share), jnp.float32),
        jnp.zeros((tok_rows, kv_count, share, HD), jnp.float32),
    )
    kv_piece = lax.all_gather(own_kv, "role", axis=0, tiled=True)
    id_piece = lax.all_gather(doc_ids[None], "role", axis=0, tiled=True)

    def one_block(entry, state):

        def take(state_in):
            block = lax.dynamic_index_in_dim(kv_piece, entry, 0, keepdims=False)
            key_ids = lax.dynamic_index_in_dim(id_piece, entry, 0, keepdims=False)
            key_side = block[0].reshape(tok_rows, kv_count, HD)
            value_side = block[1].reshape(tok_rows, kv_count, HD)
            scores = (
                jnp.einsum("qcgd,kcd->qcgk", local_q, key_side, preferred_element_type=jnp.float32)
                * scaling
            )
            key_pos = entry * tok_rows + row_steps
            visible = (key_pos[None, :] <= query_pos[:, None]) & (
                key_ids[None, :] == doc_ids[:, None]
            )
            return absorb_keys(
                state_in, scores, visible[:, None, None, :], value_side, "qcgk,kcd->qcgd"
            )

        def keep(state_in):
            return state_in

        return lax.cond(entry <= role_index, take, keep, state)

    largest, totals, summed = lax.fori_loop(0, kv_piece.shape[0], one_block, start_state)
    return (summed / totals[..., None]).astype(jnp.bfloat16).reshape(tok_rows, width_here)


def per_device(queries, keys_values, doc_ids):
    attended = head_attention(queries, keys_values, doc_ids)
    return attended


def solution(mesh):
    in_specs = (
        P(("group", "role"), "tensor"),
        P(None, ("group", "role"), None),
        P(("group", "role")),
    )
    out_specs = P(("group", "role"), "tensor")
    return jax.shard_map(
        per_device, mesh=mesh, in_specs=in_specs, out_specs=out_specs, check_vma=False
    )
```

profile of v0, /device:TPU:6, one launch (start us, length us, event | category | flops | bytes accessed | tf_op | source)
XLA Modules:
  0.0 64.0 jit_solution(12343102273541048219)
XLA Ops:
  6.5 0.0 copy-start
  6.5 0.0 copy-start.3
  6.5 0.0 all-gather.5.cloned.1.call-start
  6.5 1.6 %copy-done = bf16[2,512,1024]{2,1,0:T(8,128)(2,1)S(1)} copy-done((bf16[2,512,1024]{2,1,0:T(8,128)(2,1)S(1)}, bf16[2,512,1024]{2,1,0:T(8,128)(2,1)}, u32[]{:S(2)}) %copy-start) | copy-done | bytes 2097176
  8.1 0.9 %constant_dynamic-slice_fusion.3 = bf16[2,512,256]{2,1,0:T(8,128)(2,1)} fusion(bf16[2,512,1024]{2,1,0:T(8,128)(2,1)S(1)} %copy-done, s32[]{:T(128)S(6)} %select_n.22), kind=kLoop, calls=%fused_computation.23 | loop fusion | bytes 1048580 | tf_op jit(solution)/shard_map/dynamic_slice | solution.py:36
  9.0 0.0 all-gather.5.cloned.1.call-update
  9.0 2.3 %copy.15 = bf16[512,1024]{0,1:T(8,128)(2,1)} copy(bf16[512,1024]{1,0:T(8,128)(2,1)} %param.7) | data formatting | bytes 2097152 | tf_op args[0]
  11.3 1.6 %copy.17 = bf16[512,2,4,128]{3,0,2,1:T(8,128)(2,1)S(1)} copy(bf16[512,2,4,128]{0,3,2,1:T(8,128)(2,1)} %bitcast.46) | data formatting | bytes 2097152
  12.9 4.5 %all-gather.2 = s32[2,1,512]{2,1,0:T(1,128)S(1)} all-gather(s32[1,1,512]{2,1,0:T(1,128)} %bitcast.54), channel_id=2, replica_groups=mesh['group'=4,'tensor'=4,'role'=2] {'role'}, dimensions={0}, use_global_device_ids=true | all-gather | bytes 6144 | tf_op jit(solution)/shard_map/all_gather | solution.py:46
  17.4 13.3 %all-gather.5.cloned.1.call-done = bf16[4,512,256]{2,1,0:T(8,128)(2,1)} async-done(((bf16[2,512,256]{2,1,0:T(8,128)(2,1)}), bf16[4,512,256]{2,1,0:T(8,128)(2,1)}) %all-gather.5.cloned.1.call-update) | async-done | bytes 1048592 | tf_op jit(solution)/shard_map/all_gather | solution.py:45
  30.7 2.3 %copy.16 = bf16[2,2,512,256]{2,3,1,0:T(8,128)(2,1)} copy(bf16[2,2,512,256]{3,2,1,0:T(8,128)(2,1)} %bitcast.49) | data formatting | bytes 2097152
  33.0 1.6 %broadcast_in_dim.43 = f32[512,2,4,128]{0,3,2,1:T(8,128)} broadcast(f32[]{:T(128)} %constant.57.clone.1), dimensions={} | broadcast | bytes 2097156 | tf_op jit(solution)/shard_map/broadcast_in_dim | solution.py:43
  34.6 0.0 copy-done.3
  34.6 19.3 %while.18 = (s32[]{:T(128)}, f32[512,2,4]{0,2,1:T(4,128)S(1)}, f32[512,2,4]{0,2,1:T(4,128)S(1)}, f32[512,2,4,128]{0,3,2,1:T(8,128)}, s32[]{:T(128)}, /*index=5*/...) while((s32[]{:T(128)}, f32[512,2,4]{0,2,1:T(4,128)S(1)}, ...), condition=%wide.region_5.6_spmd.clone, body=%wide.region_0.5_spmd.clone.sunk | while | flops 1102849024 | bytes 50092432 | solution.py:72
  34.7 9.6 %conditional.3 = ((f32[512,2,4]{0,2,1:T(4,128)S(1)}, f32[512,2,4]{0,2,1:T(4,128)S(1)}, f32[512,2,4,128]{0,3,2,1:T(8,128)})) conditional(s32[]{:T(128)} %convert_element_type.21, (f32[512,2,4]{0,2,1:T(4,128)S(1)}, f32[512,2,4]{0,2,1:T(4,128)S(1)}, f32[512,2,4,128]{0,3,2,1:T(8,128)}) %tuple.49, (s32[]{:T(128)}, s32[512]{0:T(512)S(1)}, s32[]{:T(128)}, ...), branch_computations={%region_1.1_spmd, %region_2.4_spmd} | conditional | flops 1102849024 | bytes 50090148 | solution.py:70
  34.7 0.3 compare_and_fusion
  35.0 1.1 %constant_dynamic-slice_fusion.1 = (bf16[1,1,512,256]{2,3,1,0:T(8,128)(2,1)S(1)}, bf16[1,1,512,256]{2,3,1,0:T(8,128)(2,1)S(1)}) fusion(bf16[2,2,512,256]{2,3,1,0:T(8,128)(2,1)} %get-tuple-element.214, s32[]{:T(128)S(6)} %select_n.16, s32[]{:T(128)S(6)} %add.58), kind=kLoop, calls=%fused_computation.16 | loop fusion | bytes 1048584 | tf_op jit(solution)/shard_map/while/body/eval_jaxpr/cond/branch_1_fun/slice | solution.py:54
  36.1 0.0 copy-start.1
  36.1 2.1 %fusion.4 = (f32[512,2,4]{0,2,1:T(4,128)S(1)}, f32[2,512,512,4]{2,1,3,0:T(8,128)S(1)}) fusion(pred[512,512]{0,1:T(8,128)(4,1)S(1)} %compare_and_fusion, bf16[512,2,128,1]{0,2,3,1:T(8,128)(2,1)S(1)} %bitcast.42, bf16[512,2,4,128]{3,0,2,1:T(8,128)(2,1)S(1)} %get-tuple-element.215), kind=kOutput, calls=%fused_computation.4 | convolution fusion | flops 543158272 | bytes 9977856 | tf_op jit(solution)/shard_map/while/body/eval_jaxpr/cond/branch_1_fun/qcgd,kcd->qcgk/dot_general | solution.py:56
  38.2 2.0 %fusion.6 = f32[512,2,4]{0,2,1:T(4,128)S(1)} fusion(f32[2,512,512,4]{2,1,3,0:T(8,128)S(1)} %get-tuple-element.312, f32[512,2,4]{0,2,1:T(4,128)S(1)} %max.2, pred[512,512]{0,1:T(8,128)(4,1)S(1)} %compare_and_fusion), kind=kLoop, calls=%fused_computation.6 | loop fusion | flops 10481664 | bytes 8683520 | tf_op jit(solution)/shard_map/while/body/eval_jaxpr/cond/branch_1_fun/reduce_sum | solution.py:18
  40.2 0.0 copy-done.1
  40.2 2.7 %bitcast_add_fusion = f32[512,2,4,128]{0,3,2,1:T(8,128)S(1)} fusion(f32[512,2,4,128]{0,3,2,1:T(8,128)S(1)} %copy-done.1, bf16[512,2,128,1]{0,2,3,1:T(8,128)(2,1)S(1)} %bitcast.44, f32[2,512,512,4]{2,1,3,0:T(8,128)S(1)} %get-tuple-element.312, f32[512,2,4]{0,2,1:T(4,128)S(1)} %max.2, pred[512,512]{0,1:T(8,128)(4,1)S(1)} %compare_and_fusion, ...), kind=kOutput, calls=%fused_computation.9 | convolution fusion | flops 548405248 | bytes 13139968 | tf_op jit(solution)/shard_map/while/body/eval_jaxpr/cond/branch_1_fun/qcgk,kcd->qcgd/dot_general | solution.py:20
  43.0 0.0 copy-start.2
  43.0 1.3 %copy-done.2 = f32[512,2,4,128]{0,3,2,1:T(8,128)} copy-done((f32[512,2,4,128]{0,3,2,1:T(8,128)}, f32[512,2,4,128]{0,3,2,1:T(8,128)S(1)}, u32[]{:S(2)}) %copy-start.2) | copy-done | bytes 2097176 | tf_op jit(solution)/shard_map/while/body/eval_jaxpr/cond
  44.3 9.6 %conditional.3 = ((f32[512,2,4]{0,2,1:T(4,128)S(1)}, f32[512,2,4]{0,2,1:T(4,128)S(1)}, f32[512,2,4,128]{0,3,2,1:T(8,128)})) conditional(s32[]{:T(128)} %convert_element_type.21, (f32[512,2,4]{0,2,1:T(4,128)S(1)}, f32[512,2,4]{0,2,1:T(4,128)S(1)}, f32[512,2,4,128]{0,3,2,1:T(8,128)}) %tuple.49, (s32[]{:T(128)}, s32[512]{0:T(512)S(1)}, s32[]{:T(128)}, ...), branch_computations={%region_1.1_spmd, %region_2.4_spmd} | conditional | flops 1102849024 | bytes 50090148 | solution.py:70
  44.3 0.3 compare_and_fusion
  44.6 1.1 %constant_dynamic-slice_fusion.1 = (bf16[1,1,512,256]{2,3,1,0:T(8,128)(2,1)S(1)}, bf16[1,1,512,256]{2,3,1,0:T(8,128)(2,1)S(1)}) fusion(bf16[2,2,512,256]{2,3,1,0:T(8,128)(2,1)} %get-tuple-element.214, s32[]{:T(128)S(6)} %select_n.16, s32[]{:T(128)S(6)} %add.58), kind=kLoop, calls=%fused_computation.16 | loop fusion | bytes 1048584 | tf_op jit(solution)/shard_map/while/body/eval_jaxpr/cond/branch_1_fun/slice | solution.py:54
  45.7 0.0 copy-start.1
  45.7 2.1 %fusion.4 = (f32[512,2,4]{0,2,1:T(4,128)S(1)}, f32[2,512,512,4]{2,1,3,0:T(8,128)S(1)}) fusion(pred[512,512]{0,1:T(8,128)(4,1)S(1)} %compare_and_fusion, bf16[512,2,128,1]{0,2,3,1:T(8,128)(2,1)S(1)} %bitcast.42, bf16[512,2,4,128]{3,0,2,1:T(8,128)(2,1)S(1)} %get-tuple-element.215), kind=kOutput, calls=%fused_computation.4 | convolution fusion | flops 543158272 | bytes 9977856 | tf_op jit(solution)/shard_map/while/body/eval_jaxpr/cond/branch_1_fun/qcgd,kcd->qcgk/dot_general | solution.py:56
  47.8 2.0 %fusion.6 = f32[512,2,4]{0,2,1:T(4,128)S(1)} fusion(f32[2,512,512,4]{2,1,3,0:T(8,128)S(1)} %get-tuple-element.312, f32[512,2,4]{0,2,1:T(4,128)S(1)} %max.2, pred[512,512]{0,1:T(8,128)(4,1)S(1)} %compare_and_fusion), kind=kLoop, calls=%fused_computation.6 | loop fusion | flops 10481664 | bytes 8683520 | tf_op jit(solution)/shard_map/while/body/eval_jaxpr/cond/branch_1_fun/reduce_sum | solution.py:18
  49.9 0.0 copy-done.1
  49.9 2.7 %bitcast_add_fusion = f32[512,2,4,128]{0,3,2,1:T(8,128)S(1)} fusion(f32[512,2,4,128]{0,3,2,1:T(8,128)S(1)} %copy-done.1, bf16[512,2,128,1]{0,2,3,1:T(8,128)(2,1)S(1)} %bitcast.44, f32[2,512,512,4]{2,1,3,0:T(8,128)S(1)} %get-tuple-element.312, f32[512,2,4]{0,2,1:T(4,128)S(1)} %max.2, pred[512,512]{0,1:T(8,128)(4,1)S(1)} %compare_and_fusion, ...), kind=kOutput, calls=%fused_computation.9 | convolution fusion | flops 548405248 | bytes 13139968 | tf_op jit(solution)/shard_map/while/body/eval_jaxpr/cond/branch_1_fun/qcgk,kcd->qcgd/dot_general | solution.py:20
  52.6 0.0 copy-start.2
  52.6 1.3 %copy-done.2 = f32[512,2,4,128]{0,3,2,1:T(8,128)} copy-done((f32[512,2,4,128]{0,3,2,1:T(8,128)}, f32[512,2,4,128]{0,3,2,1:T(8,128)S(1)}, u32[]{:S(2)}) %copy-start.2) | copy-done | bytes 2097176 | tf_op jit(solution)/shard_map/while/body/eval_jaxpr/cond
  53.9 1.9 %divide_convert_fusion = bf16[512,2,4,128]{0,3,2,1:T(8,128)(2,1)S(1)} fusion(f32[512,2,4,128]{0,3,2,1:T(8,128)} %get-tuple-element.235, f32[512,2,4]{0,2,1:T(4,128)S(1)} %get-tuple-element.236), kind=kLoop, calls=%fused_computation.21 | loop fusion | flops 1048576 | bytes 3162112 | tf_op jit(solution)/shard_map/convert_element_type | solution.py:73
  55.8 1.3 %copy.24 = bf16[512,1024]{1,0:T(8,128)(2,1)} copy(bf16[512,1024]{0,1:T(8,128)(2,1)S(1)} %bitcast.45) | data formatting | bytes 2097152 | tf_op jit(solution)/shard_map/reshape | solution.py:73
  (15 shorter events, 0.1 us)
Async XLA Ops:
  6.5 1.6 %copy-start = (bf16[2,512,1024]{2,1,0:T(8,128)(2,1)S(1)}, bf16[2,512,1024]{2,1,0:T(8,128)(2,1)}, u32[]{:S(2)}) copy-start(bf16[2,512,1024]{2,1,0:T(8,128)(2,1)} %param.8) | copy-start | bytes 6291460
  6.5 28.1 %copy-start.3 = (s32[512]{0:T(512)S(1)}, s32[512]{0:T(512)}, u32[]{:S(2)}) copy-start(s32[512]{0:T(512)} %param.9) | copy-start | bytes 6148
  6.5 24.2 %all-gather.5.cloned.1.call-start = ((), (), s32[]{:S(2)}) async-start(), calls=%async_computation | async-start | bytes 1572864 | tf_op jit(solution)/shard_map/all_gather | solution.py:45
  36.1 4.2 %copy-start.1 = (f32[512,2,4,128]{0,3,2,1:T(8,128)S(1)}, f32[512,2,4,128]{0,3,2,1:T(8,128)}, u32[]{:S(2)}) copy-start(f32[512,2,4,128]{0,3,2,1:T(8,128)} %get-tuple-element.217) | copy-start | bytes 6291460 | tf_op jit(solution)/shard_map/while/body/eval_jaxpr/cond
  43.0 1.3 %copy-start.2 = (f32[512,2,4,128]{0,3,2,1:T(8,128)}, f32[512,2,4,128]{0,3,2,1:T(8,128)S(1)}, u32[]{:S(2)}) copy-start(f32[512,2,4,128]{0,3,2,1:T(8,128)S(1)} %bitcast_add_fusion) | copy-start | bytes 6291460 | tf_op jit(solution)/shard_map/while/body/eval_jaxpr/cond
  45.7 4.2 %copy-start.1 = (f32[512,2,4,128]{0,3,2,1:T(8,128)S(1)}, f32[512,2,4,128]{0,3,2,1:T(8,128)}, u32[]{:S(2)}) copy-start(f32[512,2,4,128]{0,3,2,1:T(8,128)} %get-tuple-element.217) | copy-start | bytes 6291460 | tf_op jit(solution)/shard_map/while/body/eval_jaxpr/cond
  52.6 1.3 %copy-start.2 = (f32[512,2,4,128]{0,3,2,1:T(8,128)}, f32[512,2,4,128]{0,3,2,1:T(8,128)S(1)}, u32[]{:S(2)}) copy-start(f32[512,2,4,128]{0,3,2,1:T(8,128)S(1)} %bitcast_add_fusion) | copy-start | bytes 6291460 | tf_op jit(solution)/shard_map/while/body/eval_jaxpr/cond
Sparse Core Ops, SparseCore 0:
  9.2 21.5 all-gather.4
where the time goes:
time: 64.2 us; the launch traced here: 64 us
  local copies, waits for them, and re-layouts  16.4 us (26%)
  between operations  13.4 us (21%)
  waiting for transfers between devices  13.3 us (21%)
  matrix products  9.54 us (15%)
  other arithmetic  6.56 us (10%)
  blocking collectives  4.5 us (7%)
    all_gather x1, waiting for transfers between devices, head_attention(): kv_piece = lax.all_gather(own_kv, 'role', axis=0, tiled=True)  13.3 us
    unnamed x8, local copies, waits for them, and re-layouts  7.75 us
    dot_general x2, matrix products, absorb_keys(): jnp.einsum(pattern, rounded, values, preferred_element_type=jnp.float32)  5.43 us
    all_gather x1, blocking collectives, head_attention(): id_piece = lax.all_gather(doc_ids[None], 'role', axis=0, tiled=True)  4.5 us
    dot_general x2, matrix products, take(): jnp.einsum('qcgd,kcd->qcgk', local_q, key_side, preferred_element_type=jn...  4.1 us
    reduce_sum x2, other arithmetic, absorb_keys(): totals = totals * factor + jnp.sum(weights, axis=-1)  4.09 us
    cond x10, local copies, waits for them, and re-layouts  2.68 us
    slice x2, local copies, waits for them, and re-layouts, take(): value_side = block[1].reshape(tok_rows, kv_count, HD)  2.14 us
  transfers between devices with their start and end apart: 1, of which 1 were waited for; matrix products, arithmetic and copies ran while one was open for 6% of the time, Pallas kernels for 0%

commit v1 on v0

--- a/solution.py
+++ b/solution.py
@@ -7,6 +7,24 @@
 HEADS = 32
 KV_HEADS = 8
 HD = 128
+
+
+def laid_out(parts, dim):
+    shape = list(parts.shape[1:])
+    shape[dim] *= parts.shape[0]
+    return jnp.moveaxis(parts, 0, dim).reshape(shape)
+
+
+def grow_blocks(x, axis):
+    peers = lax.axis_size(axis)
+    pieces = x[None]
+    for level in range(peers.bit_length() - 1):
+        bit = 1 << level
+        other = lax.ppermute(pieces, axis, [(i, i ^ bit) for i in range(peers)])
+        both = jnp.stack([pieces, other])
+        upper = lax.axis_index(axis) >> level & 1
+        pieces = jnp.where(upper == 0, both, both[::-1]).reshape(-1, *x.shape)
+    return pieces
 
 
 def absorb_keys(running, scores, visible, values, pattern):
@@ -42,7 +60,7 @@
         jnp.zeros((tok_rows, kv_count, share), jnp.float32),
         jnp.zeros((tok_rows, kv_count, share, HD), jnp.float32),
     )
-    kv_piece = lax.all_gather(own_kv, "role", axis=0, tiled=True)
+    kv_piece = laid_out(grow_blocks(own_kv, "role"), 0)
     id_piece = lax.all_gather(doc_ids[None], "role", axis=0, tiled=True)
 
     def one_block(entry, state):

time: 64.2 us -> 43.6 us (0.68)
  between operations: 13.4 us -> 0.03 us
  waiting for transfers between devices: 13.3 us -> 0.01 us
  blocking collectives: 4.5 us -> 9.61 us
  other arithmetic: 6.56 us -> 9.04 us
  local copies, waits for them, and re-layouts: 16.4 us -> 14.3 us
    all_gather x1 -> x0, waiting for transfers between devices: 13.3 us -> none  [head_attention(): kv_piece = lax.all_gather(own_kv, 'role', axis=0, tiled=True)]
    all_gather x1, blocking collectives: 4.5 us -> 9.61 us  [head_attention(): id_piece = lax.all_gather(doc_ids[None], 'role', axis=0, tiled=True)]
    another operation x0 -> x2, other arithmetic: none -> 2.47 us  [the longest x1 1.3 us: grow_blocks(): both = jnp.stack([pieces, other])]
    unnamed x8 -> x7, local copies, waits for them, and re-layouts: 7.75 us -> 5.48 us
  transfers between devices with their start and end apart: 1 -> 1, of which waited for: 1 -> 0; matrix products, arithmetic and copies ran while one was open for 6% -> 9% of each run, Pallas kernels for 0% -> 0%
where the time goes in v1:
time: 43.6 us; the launch traced here: 43.3 us
  local copies, waits for them, and re-layouts  14.3 us (33%)
  blocking collectives  9.61 us (22%)
  matrix products  9.54 us (22%)
  other arithmetic  9.04 us (21%)
  starting transfers between devices  0.53 us (1%)
    all_gather x1, blocking collectives, head_attention(): id_piece = lax.all_gather(doc_ids[None], 'role', axis=0, tiled=True)  9.61 us
    unnamed x7, local copies, waits for them, and re-layouts  5.48 us
    dot_general x2, matrix products, absorb_keys(): jnp.einsum(pattern, rounded, values, preferred_element_type=jnp.float32)  5.44 us
    dot_general x2, matrix products, take(): jnp.einsum('qcgd,kcd->qcgk', local_q, key_side, preferred_element_type=jn...  4.1 us
    reduce_sum x2, other arithmetic, absorb_keys(): totals = totals * factor + jnp.sum(weights, axis=-1)  4.09 us
    cond x10, local copies, waits for them, and re-layouts  2.7 us
    slice x2, local copies, waits for them, and re-layouts, take(): value_side = block[1].reshape(tok_rows, kv_count, HD)  2.14 us
    convert_element_type x1, other arithmetic, head_attention(): (summed / totals[..., None]).astype(jnp.bfloat16)  1.87 us
  transfers between devices with their start and end apart: 1, of which 0 were waited for; matrix products, arithmetic and copies ran while one was open for 9% of the time, Pallas kernels for 0%

profile of v1, /device:TPU:6, one launch (start us, length us, event | category | flops | bytes accessed | tf_op | source)
XLA Modules:
  0.0 43.3 jit_solution(3106117150057381736)
XLA Ops:
  0.0 0.0 copy-start
  0.0 0.0 copy-start.3
  0.0 1.6 %copy-done = bf16[2,512,1024]{2,1,0:T(8,128)(2,1)S(1)} copy-done((bf16[2,512,1024]{2,1,0:T(8,128)(2,1)S(1)}, bf16[2,512,1024]{2,1,0:T(8,128)(2,1)}, u32[]{:S(2)}) %copy-start) | copy-done | bytes 2097176
  1.6 0.1 constant_dynamic-slice_fusion.3
  1.7 1.0 %copy.17 = bf16[2,512,256]{1,2,0:T(8,128)(2,1)} copy(bf16[2,512,256]{2,1,0:T(8,128)(2,1)S(1)} %constant_dynamic-slice_fusion.3) | data formatting | bytes 1048576 | tf_op jit(solution)/shard_map/dynamic_slice | solution.py:54
  2.7 0.5 %collective-permute-start = (bf16[1,1,2,512,256]{3,4,2,1,0:T(8,128)(2,1)}, bf16[1,1,2,512,256]{3,4,2,1,0:T(8,128)(2,1)}, u32[]{:S(2)}, u32[]{:S(2)}) collective-permute-start(bf16[1,1,2,512,256]{3,4,2,1,0:T(8,128)(2,1)} %bitcast.10), channel_id=1, source_target_pairs={{0,1},{1,0},{2,3},{3,2},{4,5},{5,4},{6,7},{7,6},{8,9},{9,8},{10,11... | collective-permute-start | bytes 1572872 | tf_op jit(solution)/shard_map/ppermute | solution.py:23
  3.2 2.3 %copy.19 = bf16[512,1024]{0,1:T(8,128)(2,1)} copy(bf16[512,1024]{1,0:T(8,128)(2,1)} %param.7) | data formatting | bytes 2097152 | tf_op args[0]
  5.5 1.6 %copy.20 = bf16[512,2,4,128]{3,0,2,1:T(8,128)(2,1)S(1)} copy(bf16[512,2,4,128]{0,3,2,1:T(8,128)(2,1)} %bitcast.50) | data formatting | bytes 2097152
  7.1 9.6 %all-gather.1 = s32[2,1,512]{2,1,0:T(1,128)S(1)} all-gather(s32[1,1,512]{2,1,0:T(1,128)} %bitcast.57), channel_id=2, replica_groups=mesh['group'=4,'tensor'=4,'role'=2] {'role'}, dimensions={0}, use_global_device_ids=true | all-gather | bytes 6144 | tf_op jit(solution)/shard_map/all_gather | solution.py:64
  16.7 0.0 collective-permute-done
  16.7 1.3 %pad_maximum_fusion = bf16[2,1,1,2,512,256]{4,5,3,0,2,1:T(8,128)(2,1)S(1)} fusion(bf16[1,1,1,2,512,256]{4,5,3,0,2,1:T(8,128)(2,1)} %bitcast.11, bf16[1,1,1,2,512,256]{4,5,3,0,2,1:T(8,128)(2,1)} %bitcast.9), kind=kLoop, calls=%fused_computation.24 | loop fusion | flops 524288 | bytes 2097152 | tf_op jit(solution)/shard_map/stack | solution.py:24
  18.0 1.2 %fusion.15 = bf16[2,2,512,256]{2,3,1,0:T(8,128)(2,1)} fusion(bf16[2,1,1,2,512,256]{4,5,3,0,2,1:T(8,128)(2,1)S(1)} %pad_maximum_fusion, pred[]{:T(512)S(6)} %eq.22), kind=kLoop, calls=%fused_computation.23 | loop fusion | flops 524288 | bytes 2097153 | tf_op jit(solution)/shard_map/reshape;reshape | solution.py:15
  19.2 1.6 %broadcast_in_dim.40 = f32[512,2,4,128]{0,3,2,1:T(8,128)} broadcast(f32[]{:T(128)} %constant.58.clone.1), dimensions={} | broadcast | bytes 2097156 | tf_op jit(solution)/shard_map/broadcast_in_dim | solution.py:61
  20.8 0.0 copy-done.3
  20.8 19.3 %while.18 = (s32[]{:T(128)}, f32[512,2,4]{0,2,1:T(4,128)S(1)}, f32[512,2,4]{0,2,1:T(4,128)S(1)}, f32[512,2,4,128]{0,3,2,1:T(8,128)}, s32[]{:T(128)}, /*index=5*/...) while((s32[]{:T(128)}, f32[512,2,4]{0,2,1:T(4,128)S(1)}, ...), condition=%wide.region_5.6_spmd.clone, body=%wide.region_0.5_spmd.clone.sunk | while | flops 1102849024 | bytes 50092432 | solution.py:90
  20.8 9.7 %conditional.3 = ((f32[512,2,4]{0,2,1:T(4,128)S(1)}, f32[512,2,4]{0,2,1:T(4,128)S(1)}, f32[512,2,4,128]{0,3,2,1:T(8,128)})) conditional(s32[]{:T(128)} %convert_element_type.21, (f32[512,2,4]{0,2,1:T(4,128)S(1)}, f32[512,2,4]{0,2,1:T(4,128)S(1)}, f32[512,2,4,128]{0,3,2,1:T(8,128)}) %tuple.49, (s32[]{:T(128)}, s32[512]{0:T(512)S(1)}, s32[]{:T(128)}, ...), branch_computations={%region_1.1_spmd, %region_2.4_spmd} | conditional | flops 1102849024 | bytes 50090148 | solution.py:88
  20.9 0.3 compare_and_fusion
  21.2 1.1 %constant_dynamic-slice_fusion.1 = (bf16[1,1,512,256]{2,3,1,0:T(8,128)(2,1)S(1)}, bf16[1,1,512,256]{2,3,1,0:T(8,128)(2,1)S(1)}) fusion(bf16[2,2,512,256]{2,3,1,0:T(8,128)(2,1)} %get-tuple-element.214, s32[]{:T(128)S(6)} %select_n.22, s32[]{:T(128)S(6)} %add.58), kind=kLoop, calls=%fused_computation.16 | loop fusion | bytes 1048584 | tf_op jit(solution)/shard_map/while/body/eval_jaxpr/cond/branch_1_fun/slice | solution.py:72
  22.3 0.0 copy-start.1
  22.3 2.1 %fusion.4 = (f32[512,2,4]{0,2,1:T(4,128)S(1)}, f32[2,512,512,4]{2,1,3,0:T(8,128)S(1)}) fusion(pred[512,512]{0,1:T(8,128)(4,1)S(1)} %compare_and_fusion, bf16[512,2,128,1]{0,2,3,1:T(8,128)(2,1)S(1)} %bitcast.46, bf16[512,2,4,128]{3,0,2,1:T(8,128)(2,1)S(1)} %get-tuple-element.215), kind=kOutput, calls=%fused_computation.4 | convolution fusion | flops 543158272 | bytes 9977856 | tf_op jit(solution)/shard_map/while/body/eval_jaxpr/cond/branch_1_fun/qcgd,kcd->qcgk/dot_general | solution.py:74
  24.3 2.0 %fusion.6 = f32[512,2,4]{0,2,1:T(4,128)S(1)} fusion(f32[2,512,512,4]{2,1,3,0:T(8,128)S(1)} %get-tuple-element.312, f32[512,2,4]{0,2,1:T(4,128)S(1)} %max.2, pred[512,512]{0,1:T(8,128)(4,1)S(1)} %compare_and_fusion), kind=kLoop, calls=%fused_computation.6 | loop fusion | flops 10481664 | bytes 8683520 | tf_op jit(solution)/shard_map/while/body/eval_jaxpr/cond/branch_1_fun/reduce_sum | solution.py:36
  26.4 0.0 copy-done.1
  26.4 2.7 %bitcast_add_fusion = f32[512,2,4,128]{0,3,2,1:T(8,128)S(1)} fusion(f32[512,2,4,128]{0,3,2,1:T(8,128)S(1)} %copy-done.1, bf16[512,2,128,1]{0,2,3,1:T(8,128)(2,1)S(1)} %bitcast.48, f32[2,512,512,4]{2,1,3,0:T(8,128)S(1)} %get-tuple-element.312, f32[512,2,4]{0,2,1:T(4,128)S(1)} %max.2, pred[512,512]{0,1:T(8,128)(4,1)S(1)} %compare_and_fusion, ...), kind=kOutput, calls=%fused_computation.9 | convolution fusion | flops 548405248 | bytes 13139968 | tf_op jit(solution)/shard_map/while/body/eval_jaxpr/cond/branch_1_fun/qcgk,kcd->qcgd/dot_general | solution.py:38
  29.2 0.0 copy-start.2
  29.2 1.3 %copy-done.2 = f32[512,2,4,128]{0,3,2,1:T(8,128)} copy-done((f32[512,2,4,128]{0,3,2,1:T(8,128)}, f32[512,2,4,128]{0,3,2,1:T(8,128)S(1)}, u32[]{:S(2)}) %copy-start.2) | copy-done | bytes 2097176 | tf_op jit(solution)/shard_map/while/body/eval_jaxpr/cond
  30.5 9.6 %conditional.3 = ((f32[512,2,4]{0,2,1:T(4,128)S(1)}, f32[512,2,4]{0,2,1:T(4,128)S(1)}, f32[512,2,4,128]{0,3,2,1:T(8,128)})) conditional(s32[]{:T(128)} %convert_element_type.21, (f32[512,2,4]{0,2,1:T(4,128)S(1)}, f32[512,2,4]{0,2,1:T(4,128)S(1)}, f32[512,2,4,128]{0,3,2,1:T(8,128)}) %tuple.49, (s32[]{:T(128)}, s32[512]{0:T(512)S(1)}, s32[]{:T(128)}, ...), branch_computations={%region_1.1_spmd, %region_2.4_spmd} | conditional | flops 1102849024 | bytes 50090148 | solution.py:88
  30.5 0.3 compare_and_fusion
  30.8 1.1 %constant_dynamic-slice_fusion.1 = (bf16[1,1,512,256]{2,3,1,0:T(8,128)(2,1)S(1)}, bf16[1,1,512,256]{2,3,1,0:T(8,128)(2,1)S(1)}) fusion(bf16[2,2,512,256]{2,3,1,0:T(8,128)(2,1)} %get-tuple-element.214, s32[]{:T(128)S(6)} %select_n.22, s32[]{:T(128)S(6)} %add.58), kind=kLoop, calls=%fused_computation.16 | loop fusion | bytes 1048584 | tf_op jit(solution)/shard_map/while/body/eval_jaxpr/cond/branch_1_fun/slice | solution.py:72
  31.9 0.0 copy-start.1
  31.9 2.1 %fusion.4 = (f32[512,2,4]{0,2,1:T(4,128)S(1)}, f32[2,512,512,4]{2,1,3,0:T(8,128)S(1)}) fusion(pred[512,512]{0,1:T(8,128)(4,1)S(1)} %compare_and_fusion, bf16[512,2,128,1]{0,2,3,1:T(8,128)(2,1)S(1)} %bitcast.46, bf16[512,2,4,128]{3,0,2,1:T(8,128)(2,1)S(1)} %get-tuple-element.215), kind=kOutput, calls=%fused_computation.4 | convolution fusion | flops 543158272 | bytes 9977856 | tf_op jit(solution)/shard_map/while/body/eval_jaxpr/cond/branch_1_fun/qcgd,kcd->qcgk/dot_general | solution.py:74
  34.0 2.0 %fusion.6 = f32[512,2,4]{0,2,1:T(4,128)S(1)} fusion(f32[2,512,512,4]{2,1,3,0:T(8,128)S(1)} %get-tuple-element.312, f32[512,2,4]{0,2,1:T(4,128)S(1)} %max.2, pred[512,512]{0,1:T(8,128)(4,1)S(1)} %compare_and_fusion), kind=kLoop, calls=%fused_computation.6 | loop fusion | flops 10481664 | bytes 8683520 | tf_op jit(solution)/shard_map/while/body/eval_jaxpr/cond/branch_1_fun/reduce_sum | solution.py:36
  36.1 0.0 copy-done.1
  36.1 2.7 %bitcast_add_fusion = f32[512,2,4,128]{0,3,2,1:T(8,128)S(1)} fusion(f32[512,2,4,128]{0,3,2,1:T(8,128)S(1)} %copy-done.1, bf16[512,2,128,1]{0,2,3,1:T(8,128)(2,1)S(1)} %bitcast.48, f32[2,512,512,4]{2,1,3,0:T(8,128)S(1)} %get-tuple-element.312, f32[512,2,4]{0,2,1:T(4,128)S(1)} %max.2, pred[512,512]{0,1:T(8,128)(4,1)S(1)} %compare_and_fusion, ...), kind=kOutput, calls=%fused_computation.9 | convolution fusion | flops 548405248 | bytes 13139968 | tf_op jit(solution)/shard_map/while/body/eval_jaxpr/cond/branch_1_fun/qcgk,kcd->qcgd/dot_general | solution.py:38
  38.8 0.0 copy-start.2
  38.8 1.3 %copy-done.2 = f32[512,2,4,128]{0,3,2,1:T(8,128)} copy-done((f32[512,2,4,128]{0,3,2,1:T(8,128)}, f32[512,2,4,128]{0,3,2,1:T(8,128)S(1)}, u32[]{:S(2)}) %copy-start.2) | copy-done | bytes 2097176 | tf_op jit(solution)/shard_map/while/body/eval_jaxpr/cond
  40.1 1.9 %divide_convert_fusion = bf16[512,2,4,128]{0,3,2,1:T(8,128)(2,1)S(1)} fusion(f32[512,2,4,128]{0,3,2,1:T(8,128)} %get-tuple-element.235, f32[512,2,4]{0,2,1:T(4,128)S(1)} %get-tuple-element.236), kind=kLoop, calls=%fused_computation.21 | loop fusion | flops 1048576 | bytes 3162112 | tf_op jit(solution)/shard_map/convert_element_type | solution.py:91
  42.0 1.3 %copy.27 = bf16[512,1024]{1,0:T(8,128)(2,1)} copy(bf16[512,1024]{0,1:T(8,128)(2,1)S(1)} %bitcast.49) | data formatting | bytes 2097152 | tf_op jit(solution)/shard_map/reshape | solution.py:91
  (15 shorter events, 0.1 us)
Async XLA Ops:
  0.0 1.6 %copy-start = (bf16[2,512,1024]{2,1,0:T(8,128)(2,1)S(1)}, bf16[2,512,1024]{2,1,0:T(8,128)(2,1)}, u32[]{:S(2)}) copy-start(bf16[2,512,1024]{2,1,0:T(8,128)(2,1)} %param.8) | copy-start | bytes 6291460
  0.0 20.8 %copy-start.3 = (s32[512]{0:T(512)S(1)}, s32[512]{0:T(512)}, u32[]{:S(2)}) copy-start(s32[512]{0:T(512)} %param.9) | copy-start | bytes 6148
  2.7 14.0 %collective-permute-start = (bf16[1,1,2,512,256]{3,4,2,1,0:T(8,128)(2,1)}, bf16[1,1,2,512,256]{3,4,2,1,0:T(8,128)(2,1)}, u32[]{:S(2)}, u32[]{:S(2)}) collective-permute-start(bf16[1,1,2,512,256]{3,4,2,1,0:T(8,128)(2,1)} %bitcast.10), channel_id=1, source_target_pairs={{0,1},{1,0},{2,3},{3,2},{4,5},{5,4},{6,7},{7,6},{8,9},{9,8},{10,11... | collective-permute-start | bytes 1572872 | tf_op jit(solution)/shard_map/ppermute | solution.py:23
  22.3 4.2 %copy-start.1 = (f32[512,2,4,128]{0,3,2,1:T(8,128)S(1)}, f32[512,2,4,128]{0,3,2,1:T(8,128)}, u32[]{:S(2)}) copy-start(f32[512,2,4,128]{0,3,2,1:T(8,128)} %get-tuple-element.217) | copy-start | bytes 6291460 | tf_op jit(solution)/shard_map/while/body/eval_jaxpr/cond
  29.2 1.3 %copy-start.2 = (f32[512,2,4,128]{0,3,2,1:T(8,128)}, f32[512,2,4,128]{0,3,2,1:T(8,128)S(1)}, u32[]{:S(2)}) copy-start(f32[512,2,4,128]{0,3,2,1:T(8,128)S(1)} %bitcast_add_fusion) | copy-start | bytes 6291460 | tf_op jit(solution)/shard_map/while/body/eval_jaxpr/cond
  31.9 4.2 %copy-start.1 = (f32[512,2,4,128]{0,3,2,1:T(8,128)S(1)}, f32[512,2,4,128]{0,3,2,1:T(8,128)}, u32[]{:S(2)}) copy-start(f32[512,2,4,128]{0,3,2,1:T(8,128)} %get-tuple-element.217) | copy-start | bytes 6291460 | tf_op jit(solution)/shard_map/while/body/eval_jaxpr/cond
  38.8 1.3 %copy-start.2 = (f32[512,2,4,128]{0,3,2,1:T(8,128)}, f32[512,2,4,128]{0,3,2,1:T(8,128)S(1)}, u32[]{:S(2)}) copy-start(f32[512,2,4,128]{0,3,2,1:T(8,128)S(1)} %bitcast_add_fusion) | copy-start | bytes 6291460 | tf_op jit(solution)/shard_map/while/body/eval_jaxpr/cond
